TPU v7x, 32 devices: a whole 2x2x4 slice. The times are simulated.
32 devices in a mesh: grp: 2 (over y), tm: 4 (over z), chan: 4 (over x, core).
Axes of the slice: x: 2, y: 2, z: 4, core: 2. Of those that a mesh axis runs over, the one named last changes fastest.
Arguments:
- voltages: int32 [512, 65536], P(('grp', 'chan'), 'tm'), parts along dimension 0, may hold values from -128 to 127
- beam_delays: int32 [256, 256], replicated, may hold values from 0 to 4095
- cal_gains: float32 [2, 4096, 256], P(None, ('grp', 'tm', 'chan')), parts along dimension 1, may hold values from -4 to 4
Outputs:
- visibilities: bfloat16 [2, 4096, 256, 256], P(None, ('grp', 'tm', 'chan')), parts along dimension 1
- beam_power: bfloat16 [4096, 16, 256], P(('grp', 'tm', 'chan')), parts along dimension 0
There are 2 independent parts, one for each index of `grp`. A program takes and returns all parts, laid end to end along the dimension named above; an argument that names none is the same for every part. Nothing has to cross between parts.
All inputs are finite; a program needn't handle non-finite values.
Results may differ from a plain program's by a relative error of at most 0.0062.
Values may be sent and summed in bfloat16 or wider, within the bound.
A program may use at most 192 MiB of HBM per device.

v0:
```python
import functools
import math

import jax
import jax.numpy as jnp
import numpy as np
from jax import lax
from jax.experimental import pallas as pl
from jax.experimental.pallas import tpu as pltpu
from jax.sharding import PartitionSpec as P

TAPS = 4
FA = 64
FB = 64
NFFT = 4096
CH = 2048


def shifted(block, axis, distance):
    devices = range(lax.axis_size(axis))
    route = [(i - distance, i) for i in devices if i - distance in devices]
    return lax.ppermute(block, axis, route)


def pfb_window():
    total_len = TAPS * NFFT
    sample_pos = jnp.arange(total_len, dtype=jnp.float32)
    centre = (sample_pos - total_len / 2 + 0.5) / NFFT
    taper_win = 0.5 - 0.5 * jnp.cos(2.0 * math.pi * (sample_pos + 0.5) / total_len)
    coeffs = jnp.sinc(centre) * taper_win
    coeffs = coeffs / jnp.sqrt(jnp.sum(coeffs * coeffs))
    return coeffs.reshape(TAPS, NFFT)


RADIX = 32
LANES = NFFT // RADIX


def real_dft(rows):
    size = len(rows)
    if size == 2:
        return [(rows[0] + rows[1], None), (rows[0] - rows[1], None)]
    even, odd = real_dft(rows[0::2]), real_dft(rows[1::2])
    bins = [None] * (size // 2 + 1)
    bins[0] = (even[0][0] + odd[0][0], None)
    bins[size // 2] = (even[0][0] - odd[0][0], None)
    for k in range(1, size // 4):
        cos, sin = math.cos(2 * math.pi * k / size), math.sin(2 * math.pi * k / size)
        o_re, o_im = odd[k]
        t_re = o_re * cos + o_im * sin
        t_im = o_im * cos - o_re * sin
        bins[k] = (even[k][0] + t_re, even[k][1] + t_im)
        bins[size // 2 - k] = (even[k][0] - t_re, t_im - even[k][1])
    bins[size // 4] = (even[size // 4][0], -odd[size // 4][0])
    return bins


def twiddles():
    angle = 2.0 * np.pi * np.outer(np.arange(RADIX // 2 + 1), np.arange(LANES)) / NFFT
    table = np.stack([np.cos(angle), np.sin(angle)], axis=1).astype(np.float32)
    return np.broadcast_to(table[:, :, None, :], table.shape[:2] + (8, LANES))


def second_stage(groups):
    half = LANES // 2
    q = np.arange(LANES)
    angle = 2.0 * np.pi * (np.outer(q, q) % LANES) / LANES
    cos, sin = np.cos(angle) / 64.0, np.sin(angle) / 64.0
    real = np.concatenate([cos, sin], axis=1)
    imag = np.concatenate([-sin, cos], axis=1)
    plain = np.stack([real[:half], imag[:half]])
    mirror = np.stack([real[::-1][:half], -imag[::-1][:half]])
    none = np.zeros_like(plain)

    def ordered(first, second):
        rows = np.stack([first, second]).reshape(2, 2, groups, half // groups, 2 * LANES)
        return rows.transpose(2, 0, 1, 3, 4).reshape(2 * LANES, 2 * LANES)

    full = np.stack([ordered(plain, mirror), ordered(plain, none), ordered(none, plain)])
    high = full.astype(jnp.bfloat16)
    low = (full - high.astype(np.float64)).astype(jnp.bfloat16)
    return np.stack([high, low], axis=1)


def channelize_kernel(volt_ref, halo_ref, window_ref, twiddle_ref, dft_ref, out_ref, late, inner):
    inputs = volt_ref.shape[0]
    spectra = volt_ref.shape[1] // NFFT
    late[...] = halo_ref[...].astype(jnp.float32)

    def filter_rows(group, carry):
        first = pl.multiple_of(group * 8, 8)
        at = pl.ds(first, 8)
        for s in range(spectra):
            pieces = []
            for a in range(RADIX):
                total = None
                for tap in range(TAPS):
                    block = s + tap
                    if block < spectra:
                        col = block * NFFT + a * LANES
                        sample = volt_ref[at, col : col + LANES].astype(jnp.float32)
                    else:
                        col = (block - spectra) * NFFT + a * LANES
                        sample = late[at, col : col + LANES]
                    term = window_ref[tap, :, a * LANES : (a + 1) * LANES] * sample
                    total = term if total is None else total + term
                pieces.append(total)
            to = pl.ds(pl.multiple_of(s * inputs + first, 8), 8)
            for k, (re, im) in enumerate(real_dft(pieces)):
                cos, sin = twiddle_ref[k, 0], twiddle_ref[k, 1]
                if im is None:
                    inner[k, to, :LANES] = re * cos
                    inner[k, to, LANES:] = -re * sin
                else:
                    inner[k, to, :LANES] = re * cos + im * sin
                    inner[k, to, LANES:] = im * cos - re * sin
        return carry

    lax.fori_loop(0, inputs // 8, filter_rows, 0)

    def product(which, bins):
        over = (((1,), (1,)), ((), ()))
        dot = functools.partial(
            lax.dot_general, dimension_numbers=over, preferred_element_type=jnp.float32
        )
        high = bins.astype(jnp.bfloat16)
        low = (bins - high.astype(jnp.float32)).astype(jnp.bfloat16)
        return dot(dft_ref[which, 0], high) + (
            dot(dft_ref[which, 1], high) + dot(dft_ref[which, 0], low)
        )

    def put(k, value):
        groups, _, size, lanes = out_ref.shape
        out_ref[:, k] = value.astype(jnp.bfloat16).reshape(groups, size, lanes)

    put(0, product(1, inner[0]) + product(2, inner[RADIX // 2]))

    def transform_bin(k, carry):
        put(k, product(0, inner[k]))
        return carry

    lax.fori_loop(1, RADIX // 2, transform_bin, 0)


def channelize(voltages, halo, groups):
    inputs = voltages.shape[0]
    rows = inputs * (voltages.shape[1] // NFFT)
    window = jnp.broadcast_to(pfb_window()[:, None, :], (TAPS, 8, NFFT))
    return pl.pallas_call(
        channelize_kernel,
        out_shape=jax.ShapeDtypeStruct(
            (groups, RADIX // 2, 2 * LANES // groups, rows), jnp.bfloat16
        ),
        scratch_shapes=[
            pltpu.VMEM(halo.shape, jnp.float32),
            pltpu.VMEM((RADIX // 2 + 1, rows, 2 * LANES), jnp.float32),
        ],
        name="channelize",
    )(voltages, halo, window, twiddles(), second_stage(groups))


def exchange_kernel(out_ref, in_ref, send_sems, recv_sems, own_sem):
    tm_count, chan_count = lax.axis_size("tm"), lax.axis_size("chan")
    tm, chan = lax.axis_index("tm"), lax.axis_index("chan")
    slot = chan * tm_count + tm
    peers = []
    for tm_step in range(tm_count):
        for chan_step in range(chan_count):
            peer_tm = lax.rem(tm + tm_step, tm_count)
            peer_chan = lax.rem(chan + chan_step, chan_count)
            if tm_step or chan_step:
                peers.append((peer_tm, peer_chan))
    barrier = pltpu.get_barrier_semaphore()
    for peer_tm, peer_chan in peers:
        pl.semaphore_signal(
            barrier,
            inc=1,
            device_id={"tm": peer_tm, "chan": peer_chan},
            device_id_type=pl.DeviceIdType.MESH,
        )
    pl.semaphore_wait(barrier, len(peers))
    copies = []
    for index, (peer_tm, peer_chan) in enumerate(peers):
        copy = pltpu.make_async_remote_copy(
            src_ref=out_ref.at[peer_tm * chan_count + peer_chan],
            dst_ref=in_ref.at[slot],
            send_sem=send_sems.at[index],
            recv_sem=recv_sems.at[index],
            device_id={"tm": peer_tm, "chan": peer_chan},
            device_id_type=pl.DeviceIdType.MESH,
        )
        copy.start()
        copies.append(copy)
    own = pltpu.make_async_copy(out_ref.at[tm * chan_count + chan], in_ref.at[slot], own_sem)
    own.start()
    own.wait()
    for copy in copies:
        copy.wait()


def exchange(bins):
    return pl.pallas_call(
        exchange_kernel,
        in_specs=[pl.BlockSpec(memory_space=pl.ANY)],
        out_specs=pl.BlockSpec(memory_space=pl.ANY),
        out_shape=jax.ShapeDtypeStruct(bins.shape, bins.dtype),
        scratch_shapes=[
            pltpu.SemaphoreType.DMA((bins.shape[0] - 1,)),
            pltpu.SemaphoreType.DMA((bins.shape[0] - 1,)),
            pltpu.SemaphoreType.DMA,
        ],
        compiler_params=pltpu.CompilerParams(collective_id=0, has_side_effects=True),
        name="exchange",
    )(bins)


def correlate_bins_kernel(
    bins_ref, gain_ref, delay_ref, vis_ref, power_ref,
    cur_re, cur_im, rot_re, rot_im, far_re, far_im, w_re, w_im, rows_buf, power_buf,
):
    k1 = pl.program_id(0)
    tm_count, chan_count = lax.axis_size("tm"), lax.axis_size("chan")
    sources, _, size, lanes = bins_ref.shape
    block = vis_ref.shape[1]
    inputs = vis_ref.shape[4]
    own_inputs = inputs // chan_count
    spec_dev = lanes // own_inputs
    spectra = spec_dev * tm_count

    @pl.when(k1 == 0)
    def _():
        first = (lax.axis_index("tm") * chan_count + lax.axis_index("chan")) * (block * RADIX)
        delays = delay_ref[...].T
        norm = 1.0 / math.sqrt(inputs)

        def phase(steps):
            return (delays * steps % NFFT).astype(jnp.float32) * (2.0 * math.pi / NFFT)

        cur_re[...] = jnp.cos(phase(first)) * norm
        cur_im[...] = -jnp.sin(phase(first)) * norm
        rot_re[...] = jnp.cos(phase(1))
        rot_im[...] = -jnp.sin(phase(1))
        far_re[...] = jnp.cos(phase(RADIX))
        far_im[...] = -jnp.sin(phase(RADIX))

    rows = 16

    def advance(chunk, carry):
        at = pl.ds(pl.multiple_of(chunk * rows, rows), rows)
        c_re, c_im = cur_re[at, :], cur_im[at, :]
        r_re, r_im = rot_re[at, :], rot_im[at, :]
        cur_re[at, :] = c_re * r_re - c_im * r_im
        cur_im[at, :] = c_re * r_im + c_im * r_re
        r_re, r_im = far_re[at, :], far_im[at, :]
        for q in range(block):
            w_re[q, at, :] = c_re.astype(jnp.bfloat16)
            w_im[q, at, :] = c_im.astype(jnp.bfloat16)
            if q + 1 < block:
                c_re, c_im = c_re * r_re - c_im * r_im, c_re * r_im + c_im * r_re
        return carry

    lax.fori_loop(0, inputs // rows, advance, 0, unroll=True)

    received = bins_ref[...].astype(jnp.float32).reshape(sources * size, lanes)
    for part in range(lanes // LANES):
        rows_buf[part] = received[:, part * LANES : (part + 1) * LANES]
    mirror = jnp.where(k1 >= RADIX // 2, size // 2, 0)

    def gathered(row):
        parts = []
        for chan in range(chan_count):
            at = pl.ds(chan * tm_count * size + mirror + row, tm_count, stride=size)
            pieces = [rows_buf[part, at, :] for part in range(lanes // LANES)]
            parts.append(jnp.concatenate(pieces, axis=1))
        return jnp.concatenate(
            [
                jnp.concatenate([p[:, s * own_inputs : (s + 1) * own_inputs] for p in parts], axis=1)
                for s in range(spec_dev)
            ],
            axis=0,
        )

    g_re_all, g_im_all = gain_ref[0, :, 0], gain_ref[1, :, 0]
    for q in range(block):
        a_re, a_im = gathered(q), gathered(block + q)
        g_re, g_im = g_re_all[q], g_im_all[q]
        cal_re = (g_re * a_re - g_im * a_im).astype(jnp.bfloat16)
        cal_im = (g_re * a_im + g_im * a_re).astype(jnp.bfloat16)
        stacked = jnp.concatenate([cal_re, cal_im], axis=0)
        flipped = jnp.concatenate([cal_im, -cal_re], axis=0)
        over_time = (((0,), (0,)), ((), ()))
        for part, left in enumerate((stacked, flipped)):
            vis = lax.dot_general(left, stacked, over_time, preferred_element_type=jnp.float32)
            vis_ref[part, q, 0] = (vis * (1.0 / spectra)).astype(jnp.bfloat16)
        by_re = jnp.dot(stacked, w_re[q], preferred_element_type=jnp.float32)
        by_im = jnp.dot(stacked, w_im[q], preferred_element_type=jnp.float32)
        beam_re = by_re[:spectra] - by_im[spectra:]
        beam_im = by_re[spectra:] + by_im[:spectra]
        power = beam_re * beam_re + beam_im * beam_im
        for part in range(power.shape[1] // LANES):
            cols = slice(part * LANES, (part + 1) * LANES)
            power_buf[q, part] = power[:, cols]
            in_order = [
                power_buf[q, part, pl.ds(t, spec_dev, stride=tm_count), :] for t in range(tm_count)
            ]
            power_ref[q, 0, :, cols] = jnp.concatenate(in_order, axis=0).astype(jnp.bfloat16)


def correlate_bins(bins, beam_delays, cal_gains):
    sources, half, size, lanes = bins.shape
    _, chan_local, inputs = cal_gains.shape
    beams = beam_delays.shape[0]
    block = chan_local // RADIX
    spectra = sources * lanes // inputs
    table = pltpu.VMEM((inputs, beams), jnp.float32)
    vis, power = pl.pallas_call(
        correlate_bins_kernel,
        grid=(RADIX,),
        in_specs=[
            pl.BlockSpec(
                (sources, 1, size, lanes),
                lambda k: (0, jnp.where(k > half, RADIX - k, lax.rem(k, half)), 0, 0),
            ),
            pl.BlockSpec((2, block, 1, 1, inputs), lambda k: (0, 0, k, 0, 0)),
            pl.BlockSpec((beams, inputs), lambda k: (0, 0)),
        ],
        out_specs=[
            pl.BlockSpec((2, block, 1, inputs, inputs), lambda k: (0, 0, k, 0, 0)),
            pl.BlockSpec((block, 1, spectra, beams), lambda k: (0, k, 0, 0)),
        ],
        out_shape=[
            jax.ShapeDtypeStruct((2, block, RADIX, inputs, inputs), jnp.bfloat16),
            jax.ShapeDtypeStruct((block, RADIX, spectra, beams), jnp.bfloat16),
        ],
        scratch_shapes=[table] * 6
        + [pltpu.VMEM((block, inputs, beams), jnp.bfloat16)] * 2
        + [
            pltpu.VMEM((lanes // LANES, sources * size, LANES), jnp.float32),
            pltpu.VMEM((block, beams // LANES, spectra, LANES), jnp.float32),
        ],
        compiler_params=pltpu.CompilerParams(dimension_semantics=("arbitrary",)),
        name="correlate",
    )(bins, cal_gains.reshape(2, block, RADIX, 1, inputs), beam_delays)
    return (
        vis.reshape(2, chan_local, inputs, inputs),
        power.reshape(chan_local, spectra, beams),
    )


def correlate_kernel(
    spec_ref, gain_ref, delay_ref, vis_ref, power_ref, cur_re, cur_im, rot_re, rot_im, w_re, w_im
):
    step = pl.program_id(0)
    block = spec_ref.shape[1]
    spectra = spec_ref.shape[2]
    inputs = spec_ref.shape[3]
    beams = delay_ref.shape[0]

    @pl.when(step == 0)
    def _():
        chan_count = lax.axis_size("chan")
        first = (lax.axis_index("tm") * chan_count + lax.axis_index("chan")) * (
            block * pl.num_programs(0)
        )
        delays = delay_ref[...].T
        start = (delays * first % NFFT).astype(jnp.float32) * (2.0 * math.pi / NFFT)
        turn = delays.astype(jnp.float32) * (2.0 * math.pi / NFFT)
        norm = 1.0 / math.sqrt(inputs)
        cur_re[...] = jnp.cos(start) * norm
        cur_im[...] = -jnp.sin(start) * norm
        rot_re[...] = jnp.cos(turn)
        rot_im[...] = -jnp.sin(turn)

    rows = 16

    def advance(chunk, carry):
        at = pl.ds(pl.multiple_of(chunk * rows, rows), rows)
        c_re, c_im = cur_re[at, :], cur_im[at, :]
        r_re, r_im = rot_re[at, :], rot_im[at, :]
        for c in range(block):
            w_re[c, at, :] = c_re.astype(jnp.bfloat16)
            w_im[c, at, :] = c_im.astype(jnp.bfloat16)
            c_re, c_im = c_re * r_re - c_im * r_im, c_re * r_im + c_im * r_re
        cur_re[at, :] = c_re
        cur_im[at, :] = c_im
        return carry

    lax.fori_loop(0, inputs // rows, advance, 0, unroll=True)

    for c in range(block):
        a_re = spec_ref[0, c].astype(jnp.float32)
        a_im = spec_ref[1, c].astype(jnp.float32)
        g_re = gain_ref[0, c : c + 1, :]
        g_im = gain_ref[1, c : c + 1, :]
        cal_re = (g_re * a_re - g_im * a_im).astype(jnp.bfloat16)
        cal_im = (g_re * a_im + g_im * a_re).astype(jnp.bfloat16)
        stacked = jnp.concatenate([cal_re, cal_im], axis=0)
        flipped = jnp.concatenate([cal_im, -cal_re], axis=0)
        over_time = (((0,), (0,)), ((), ()))
        for part, left in enumerate((stacked, flipped)):
            vis = lax.dot_general(left, stacked, over_time, preferred_element_type=jnp.float32)
            vis_ref[part, c] = (vis * (1.0 / spectra)).astype(jnp.bfloat16)
        by_re = jnp.dot(stacked, w_re[c], preferred_element_type=jnp.float32)
        by_im = jnp.dot(stacked, w_im[c], preferred_element_type=jnp.float32)
        beam_re = by_re[:spectra] - by_im[spectra:]
        beam_im = by_re[spectra:] + by_im[:spectra]
        power_ref[c] = (beam_re * beam_re + beam_im * beam_im).astype(jnp.bfloat16)


def correlate(spectra, beam_delays, cal_gains):
    _, chan_local, spectra_total, inputs = spectra.shape
    beams = beam_delays.shape[0]
    block = math.gcd(chan_local, 8)
    table = pltpu.VMEM((inputs, beams), jnp.float32)
    return pl.pallas_call(
        correlate_kernel,
        grid=(chan_local // block,),
        in_specs=[
            pl.BlockSpec((2, block, spectra_total, inputs), lambda g: (0, g, 0, 0)),
            pl.BlockSpec((2, block, inputs), lambda g: (0, g, 0)),
            pl.BlockSpec((beams, inputs), lambda g: (0, 0)),
        ],
        out_specs=[
            pl.BlockSpec((2, block, inputs, inputs), lambda g: (0, g, 0, 0)),
            pl.BlockSpec((block, spectra_total, beams), lambda g: (g, 0, 0)),
        ],
        out_shape=[
            jax.ShapeDtypeStruct((2, chan_local, inputs, inputs), jnp.bfloat16),
            jax.ShapeDtypeStruct((chan_local, spectra_total, beams), jnp.bfloat16),
        ],
        scratch_shapes=[table] * 4 + [pltpu.VMEM((block, inputs, beams), jnp.bfloat16)] * 2,
        compiler_params=pltpu.CompilerParams(dimension_semantics=("arbitrary",)),
        name="correlate",
    )(spectra, cal_gains, beam_delays)


def shards(voltages, beam_delays, cal_gains):
    inp_dev = voltages.shape[0]
    spec_dev = voltages.shape[1] // NFFT
    tm_count = lax.axis_size("tm")
    chan_count = lax.axis_size("chan")
    spectra_total = spec_dev * tm_count
    halo = shifted(voltages[:, : (TAPS - 1) * NFFT].astype(jnp.bfloat16), "tm", -1)
    devices = tm_count * chan_count
    if CH % (4 * RADIX * devices) == 0:
        bins = exchange(channelize(voltages, halo, devices))
        return correlate_bins(bins, beam_delays, cal_gains)
    half = LANES // 2
    bins = channelize(voltages, halo, half).reshape(RADIX // 2, half, 2, 2, spec_dev, inp_dev)
    plain, mirror = bins[:, :, 0], bins[:, :, 1]
    bins = jnp.concatenate([plain, mirror[:1], mirror[:0:-1]], axis=0)
    packed = bins.transpose(2, 1, 0, 3, 4).reshape(2, CH, spec_dev, inp_dev)
    chan_local = CH // (tm_count * chan_count)
    reordered = packed.reshape(2, tm_count, chan_count, chan_local, spec_dev, inp_dev)
    reordered = reordered.transpose(0, 2, 1, 3, 4, 5).reshape(2, CH, spec_dev, inp_dev)
    sectioned = lax.all_to_all(reordered, "chan", split_axis=1, concat_axis=3, tiled=True)
    turned = lax.all_to_all(sectioned, "tm", split_axis=1, concat_axis=2, tiled=True)
    return correlate(turned, beam_delays, cal_gains)


def solution(mesh):
    return jax.shard_map(
        shards,
        mesh=mesh,
        in_specs=(P(("grp", "chan"), "tm"), P(), P(None, ("grp", "tm", "chan"), None)),
        out_specs=(
            P(None, ("grp", "tm", "chan"), None, None),
            P(("grp", "tm", "chan"), None, None),
        ),
        check_vma=False,
    )
```

profile of v0, /device:TPU:9, one launch (start us, length us, event | category | flops | bytes accessed | tf_op | source)
XLA Modules:
  0.0 140.9 jit_solution(12050398173309754797)
XLA Ops:
  0.6 0.0 copy-start.2
  0.6 0.0 copy-start.1
  0.7 2.1 %slice_convert_fusion = bf16[64,12288]{1,0:T(8,128)(2,1)S(1)} fusion(s32[64,16384]{1,0:T(8,128)} %volt_ref.1), kind=kLoop, calls=%fused_computation | loop fusion | flops 786432 | bytes 4718592 | tf_op jit(solution)/shard_map/convert
  2.7 1.9 %collective-permute-start = (bf16[64,12288]{1,0:T(8,128)(2,1)S(1)}, bf16[64,12288]{1,0:T(8,128)(2,1)S(1)}, u32[]{:S(2)}, u32[]{:S(2)}) collective-permute-start(bf16[64,12288]{1,0:T(8,128)(2,1)S(1)} %slice_convert_fusion), channel_id=1, source_target_pairs={{4,0},{8,4},{12,8},{5,1},{9,5},{13,9},{6,2},{10,6},{14,10},{7,3},{... | collective-permute-start | bytes 4718600 | tf_op jit(solution)/shard_map/ppermute | solution.py:22
  4.7 0.9 fusion.42
  6.3 0.0 copy-done.1
  6.3 1.0 reshape.63.gain_ref
  7.3 0.6 fusion.15
  7.9 32.0 %collective-permute-done.halo_ref = bf16[64,12288]{1,0:T(8,128)(2,1)S(1)} collective-permute-done((bf16[64,12288]{1,0:T(8,128)(2,1)S(1)}, bf16[64,12288]{1,0:T(8,128)(2,1)S(1)}, u32[]{:S(2)}, u32[]{:S(2)}) %collective-permute-start) | collective-permute-done | bytes 1572896 | tf_op jit(solution)/shard_map/ppermute | solution.py:22
  39.9 0.0 copy-start
  39.9 0.9 broadcast_in_dim.10.window_ref
  40.8 0.0 copy-done.2
  40.8 0.7 jit_solution_.3.twiddle_ref
  41.5 0.0 copy-done
  41.5 12.4 %channelize.1.out_ref = bf16[16,16,16,256]{3,2,1,0:T(8,128)(2,1)} custom-call(s32[64,16384]{1,0:T(8,128)} %volt_ref.1, bf16[64,12288]{1,0:T(8,128)(2,1)} %copy-done, f32[4,8,4096]{2,1,0:T(8,128)} %broadcast_in_dim.10.window_ref, f32[17,2,8,128]{3,2,1,0:T(8,128)} %jit_solution_.3.twiddle_ref, bf16[3,2,256,256]{3,2,1,0:T(8,128)(2,1)} %constant.69.clone.dft_ref), custom_call_target="tpu_custom_call" | custom-call | tf_op jit(solution)/shard_map/channelize/pallas_call | solution.py:149
  53.8 50.5 %exchange.1.bins_ref = bf16[16,16,16,256]{3,2,1,0:T(8,128)(2,1)} custom-call(bf16[16,16,16,256]{3,2,1,0:T(8,128)(2,1)} %channelize.1.out_ref), custom_call_target="tpu_custom_call" | custom-call | tf_op jit(solution)/shard_map/exchange/pallas_call | solution.py:202
  104.3 36.6 %correlate.1 = (bf16[2,4,32,256,256]{4,3,2,1,0:T(8,128)(2,1)}, bf16[4,32,16,256]{3,2,1,0:T(8,128)(2,1)}) custom-call(bf16[16,16,16,256]{3,2,1,0:T(8,128)(2,1)} %exchange.1.bins_ref, f32[2,4,32,1,256]{4,3,2,1,0:T(1,128)} %reshape.63.gain_ref, s32[256,256]{1,0:T(8,128)} %delay_ref.1), custom_call_target="tpu_custom_call" | custom-call | tf_op jit(solution)/shard_map/correlate/pallas_call | solution.py:316
Async XLA Ops:
  0.6 40.2 %copy-start.2 = (f32[17,2,128]{2,1,0:T(2,128)S(1)}, f32[17,2,128]{2,1,0:T(2,128)}, u32[]{:S(2)}) copy-start(f32[17,2,128]{2,1,0:T(2,128)} %constant.68.clone) | copy-start | bytes 52228
  0.6 5.7 %copy-start.1 = (f32[2,128,256]{2,1,0:T(8,128)S(1)}, f32[2,128,256]{2,1,0:T(8,128)}, u32[]{:S(2)}) copy-start(f32[2,128,256]{2,1,0:T(8,128)} %param.7) | copy-start | bytes 786436
  2.7 37.2 %collective-permute-start = (bf16[64,12288]{1,0:T(8,128)(2,1)S(1)}, bf16[64,12288]{1,0:T(8,128)(2,1)S(1)}, u32[]{:S(2)}, u32[]{:S(2)}) collective-permute-start(bf16[64,12288]{1,0:T(8,128)(2,1)S(1)} %slice_convert_fusion), channel_id=1, source_target_pairs={{4,0},{8,4},{12,8},{5,1},{9,5},{13,9},{6,2},{10,6},{14,10},{7,3},{... | collective-permute-start | bytes 4718600 | tf_op jit(solution)/shard_map/ppermute | solution.py:22
  39.9 1.5 %copy-start = (bf16[64,12288]{1,0:T(8,128)(2,1)}, bf16[64,12288]{1,0:T(8,128)(2,1)S(1)}, u32[]{:S(2)}) copy-start(bf16[64,12288]{1,0:T(8,128)(2,1)S(1)} %collective-permute-done.halo_ref) | copy-start | bytes 4718596
where the time goes:
time: 142 us; the launch traced here: 141 us
  Pallas kernels  99.5 us (70%)
  waiting for transfers between devices  32 us (23%)
  other arithmetic  3.66 us (3%)
  local copies, waits for them, and re-layouts  2.54 us (2%)
  starting transfers between devices  1.92 us (1%)
    pallas_call x1, Pallas kernels, exchange(): pl.pallas_call(exchange_kernel, in_specs=[pl.BlockSpec(memory_space=pl.AN...  50.5 us
    pallas_call x1, Pallas kernels, correlate_bins(): pl.pallas_call(correlate_bins_kernel, grid=(RADIX,), in_specs=[pl.BlockSp...  36.6 us
    ppermute x1, waiting for transfers between devices, shifted(): return lax.ppermute(block, axis, route)  32 us
    pallas_call x1, Pallas kernels, channelize(): pl.pallas_call(channelize_kernel, out_shape=jax.ShapeDtypeStruct((groups,...  12.4 us
  transfers between devices with their start and end apart: 1, of which 1 were waited for; matrix products, arithmetic and copies ran while one was open for 2% of the time, Pallas kernels for 0%

commit v1 on v0

--- a/solution.py
+++ b/solution.py
@@ -159,192 +159,320 @@
     )(voltages, halo, window, twiddles(), second_stage(groups))
 
 
-def exchange_kernel(out_ref, in_ref, send_sems, recv_sems, own_sem):
+def window_table():
+    total_len = TAPS * NFFT
+    pos = np.arange(total_len, dtype=np.float64)
+    taper_win = 0.5 - 0.5 * np.cos(2.0 * np.pi * (pos + 0.5) / total_len)
+    coeffs = np.sinc((pos - total_len / 2 + 0.5) / NFFT) * taper_win
+    coeffs = coeffs / np.sqrt(np.sum(coeffs * coeffs))
+    return coeffs.reshape(TAPS, RADIX, LANES).astype(np.float32)
+
+
+def twiddle_table():
+    angle = 2.0 * np.pi * np.outer(np.arange(RADIX // 2 + 1), np.arange(LANES)) / NFFT
+    return np.stack([np.cos(angle), np.sin(angle)], axis=1).astype(np.float32)
+
+
+MESH = pl.DeviceIdType.MESH
+HALO = TAPS - 1
+PAIRS = RADIX // 4
+LATE = 2
+CHUNKS = 4
+
+
+def spectra_kernel(
+    volt_ref, window_ref, twiddle_ref, dft_ref, gain_ref, cal_ref,
+    blocks, win, turn, filtered, inner, inner_last, send, recv, rows_buf,
+    halo_send, halo_recv, send_sems, early_sem, late_sems,
+):
     tm_count, chan_count = lax.axis_size("tm"), lax.axis_size("chan")
     tm, chan = lax.axis_index("tm"), lax.axis_index("chan")
-    slot = chan * tm_count + tm
-    peers = []
+    inputs = volt_ref.shape[0]
+    spec_dev = volt_ref.shape[1] // NFFT
+    slots = send.shape[0]
+    devices = tm_count * chan_count
+    last = tm_count - 1
+
+    barrier = pltpu.get_barrier_semaphore()
     for tm_step in range(tm_count):
         for chan_step in range(chan_count):
-            peer_tm = lax.rem(tm + tm_step, tm_count)
-            peer_chan = lax.rem(chan + chan_step, chan_count)
             if tm_step or chan_step:
-                peers.append((peer_tm, peer_chan))
-    barrier = pltpu.get_barrier_semaphore()
-    for peer_tm, peer_chan in peers:
-        pl.semaphore_signal(
-            barrier,
-            inc=1,
-            device_id={"tm": peer_tm, "chan": peer_chan},
-            device_id_type=pl.DeviceIdType.MESH,
+                peer = {
+                    "tm": lax.rem(tm + tm_step, tm_count),
+                    "chan": lax.rem(chan + chan_step, chan_count),
+                }
+                pl.semaphore_signal(barrier, inc=1, device_id=peer, device_id_type=MESH)
+
+    def load_block(b):
+        def column(a, carry):
+            col = pl.multiple_of(b * NFFT + a * LANES, LANES)
+            blocks[HALO + b, a] = (
+                volt_ref[:, pl.ds(col, LANES)].astype(jnp.float32).astype(jnp.bfloat16)
+            )
+            return carry
+
+        lax.fori_loop(0, RADIX, column, 0)
+
+    def halo_copy(h):
+        return pltpu.make_async_remote_copy(
+            src_ref=blocks.at[spec_dev + h],
+            dst_ref=blocks.at[h],
+            send_sem=halo_send.at[h],
+            recv_sem=halo_recv.at[h],
+            device_id={"tm": jnp.minimum(tm + 1, last)},
+            device_id_type=MESH,
         )
-    pl.semaphore_wait(barrier, len(peers))
-    copies = []
-    for index, (peer_tm, peer_chan) in enumerate(peers):
-        copy = pltpu.make_async_remote_copy(
-            src_ref=out_ref.at[peer_tm * chan_count + peer_chan],
-            dst_ref=in_ref.at[slot],
-            send_sem=send_sems.at[index],
-            recv_sem=recv_sems.at[index],
-            device_id={"tm": peer_tm, "chan": peer_chan},
-            device_id_type=pl.DeviceIdType.MESH,
+
+    for h in reversed(range(HALO)):
+        load_block(spec_dev - HALO + h)
+
+    pl.semaphore_wait(barrier, devices - 1)
+
+    @pl.when(tm < last)
+    def _():
+        for h in reversed(range(HALO)):
+            halo_copy(h).start()
+
+    for b in range(spec_dev - HALO):
+        load_block(b)
+
+    @pl.when(tm == last)
+    def _():
+        def clear(a, carry):
+            for b in range(HALO):
+                blocks[HALO + spec_dev + b, a] = jnp.zeros((inputs, LANES), jnp.bfloat16)
+            return carry
+
+        lax.fori_loop(0, RADIX, clear, 0)
+
+    def spread(a, carry):
+        for tap in range(TAPS):
+            win[tap, a] = jnp.broadcast_to(window_ref[tap, pl.ds(a, 1), :], (8, LANES))
+        return carry
+
+    lax.fori_loop(0, RADIX, spread, 0)
+    for k in range(RADIX // 2 + 1):
+        for part in range(2):
+            turn[k, part] = jnp.broadcast_to(twiddle_ref[k, part : part + 1, :], (8, LANES))
+
+    def product(which, bins):
+        over = (((1,), (1,)), ((), ()))
+        dot = functools.partial(
+            lax.dot_general, dimension_numbers=over, preferred_element_type=jnp.float32
         )
-        copy.start()
-        copies.append(copy)
-    own = pltpu.make_async_copy(out_ref.at[tm * chan_count + chan], in_ref.at[slot], own_sem)
-    own.start()
-    own.wait()
-    for copy in copies:
-        copy.wait()
-
-
-def exchange(bins):
+        high = bins.astype(jnp.bfloat16)
+        low = (bins - high.astype(jnp.float32)).astype(jnp.bfloat16)
+        return dot(dft_ref[which, 0], high) + (
+            dot(dft_ref[which, 1], high) + dot(dft_ref[which, 0], low)
+        )
+
+    def transform(slot):
+        def filter_column(a, carry):
+            taps = [win[tap, a] for tap in range(TAPS)]
+            for row in range(0, inputs, 16):
+                total = None
+                for tap in range(TAPS):
+                    sample = blocks[slot + tap, a, row : row + 16].astype(jnp.float32)
+                    term = taps[tap][None] * sample.reshape(2, 8, LANES)
+                    total = term if total is None else total + term
+                filtered[a, row : row + 16] = total.reshape(16, LANES)
+            return carry
+
+        lax.fori_loop(0, RADIX, filter_column, 0)
+
+        def first_stage(group, carry):
+            at = pl.ds(pl.multiple_of(group * 8, 8), 8)
+            upper = pl.ds(pl.multiple_of(inputs + group * 8, 8), 8)
+            pieces = [filtered[a, at] for a in range(RADIX)]
+            for k, (re, im) in enumerate(real_dft(pieces)):
+                cos, sin = turn[k, 0], turn[k, 1]
+                if im is None:
+                    o_re, o_im = re * cos, -re * sin
+                else:
+                    o_re, o_im = re * cos + im * sin, im * cos - re * sin
+                if k == RADIX // 2:
+                    inner_last[at, :LANES] = o_re
+                    inner_last[at, LANES:] = o_im
+                else:
+                    rows = at if k < PAIRS else upper
+                    inner[k % PAIRS, rows, :LANES] = o_re
+                    inner[k % PAIRS, rows, LANES:] = o_im
+            return carry
+
+        lax.fori_loop(0, inputs // 8, first_stage, 0)
+
+        def put(pair, value):
+            send[slot, :, pair] = value.astype(jnp.bfloat16).reshape(devices, -1, LANES)
+
+        first = product(1, inner[0, :inputs]) + product(2, inner_last[...])
+        put(0, jnp.concatenate([first, product(0, inner[0, inputs:])], axis=1))
+
+        def second(pair, carry):
+            put(pair, product(0, inner[pair]))
+            return carry
+
+        lax.fori_loop(1, PAIRS, second, 0)
+
+    def deliver(slot, pairs, sem):
+        at = spec_dev * tm - HALO + slot
+        for i in range(tm_count):
+            peer_tm = jnp.where(2 * tm >= tm_count, i, last - i)
+            for step in range(chan_count):
+                peer_chan = lax.rem(chan + step, chan_count)
+                src = send.at[slot, peer_tm * chan_count + peer_chan, pairs]
+                dst = recv.at[chan, at, pairs]
+
+                def remote(src=src, dst=dst, peer_tm=peer_tm, peer_chan=peer_chan):
+                    pltpu.make_async_remote_copy(
+                        src_ref=src,
+                        dst_ref=dst,
+                        send_sem=send_sems.at[slot],
+                        recv_sem=sem,
+                        device_id={"tm": peer_tm, "chan": peer_chan},
+                        device_id_type=MESH,
+                    ).start()
+
+                if step:
+                    remote()
+                else:
+                    pl.when(peer_tm != tm)(remote)
+
+                    @pl.when(peer_tm == tm)
+                    def _(src=src, dst=dst):
+                        pltpu.make_async_copy(src, dst, sem).start()
+
+    def run(slot):
+        transform(slot)
+
+        @pl.when(slot >= LATE)
+        def _():
+            deliver(slot, pl.ds(0, PAIRS), early_sem)
+
+    def forward(step, carry):
+        slot = step + HALO
+
+        @pl.when(jnp.logical_or(slot < spec_dev, tm == last))
+        def _():
+            run(slot)
+
+        return carry
+
+    lax.fori_loop(0, spec_dev, forward, 0)
+
+    def backward(step, carry):
+        slot = HALO - 1 - step
+
+        @pl.when(tm > 0)
+        def _():
+            halo_copy(slot).wait_recv()
+            run(slot)
+
+        return carry
+
+    lax.fori_loop(0, HALO, backward, 0)
+
+    size = PAIRS // CHUNKS
+
+    @pl.when(tm > 0)
+    def _():
+        def piece(chunk, carry):
+            for slot in reversed(range(LATE)):
+                deliver(slot, pl.ds(chunk * size, size), late_sems.at[chunk])
+            return carry
+
+        lax.fori_loop(0, CHUNKS, piece, 0)
+
+    late = LATE * last
+    early = tm_count * spec_dev - late
+
+    def drain(ref, sem):
+        pltpu.make_async_copy(ref, ref, sem).wait()
+
+    drain(recv.at[:, pl.ds(0, early)], early_sem)
+
+    spectra = tm_count * spec_dev
+    rows = 2 * LANES // devices
+    block = rows // 4
+
+    def calibrate(chunk, carry):
+        drain(recv.at[:, pl.ds(0, late), pl.ds(chunk * size, size)], late_sems.at[chunk])
+        for part in range(size):
+            pair = chunk * size + part
+            for c in range(chan_count):
+                rows_buf[c] = recv[c, :, pair].astype(jnp.float32).reshape(spectra * rows, LANES)
+            for mirror in range(2):
+                for q in range(block):
+                    row = 2 * block * mirror + q
+                    pick = lambda r: [
+                        rows_buf[c, pl.ds(r, spectra, stride=rows), :] for c in range(chan_count)
+                    ]
+                    all_re, all_im = pick(row), pick(row + block)
+                    for half in range(2):
+                        cols = slice(half * inputs, (half + 1) * inputs)
+                        a_re = jnp.concatenate([v[:, cols] for v in all_re], axis=1)
+                        a_im = jnp.concatenate([v[:, cols] for v in all_im], axis=1)
+                        k = pair + half * PAIRS
+                        if mirror:
+                            k = jnp.where(k == 0, RADIX // 2, RADIX - k)
+                        channel = q * RADIX + k
+                        g_re = gain_ref[0, pl.ds(channel, 1), :]
+                        g_im = gain_ref[1, pl.ds(channel, 1), :]
+                        cal_re = (g_re * a_re - g_im * a_im).astype(jnp.bfloat16)
+                        cal_im = (g_re * a_im + g_im * a_re).astype(jnp.bfloat16)
+                        cal_ref[channel, :spectra] = cal_re
+                        cal_ref[channel, spectra:] = cal_im
+        return carry
+
+    lax.fori_loop(0, CHUNKS, calibrate, 0)
+
+    @pl.when(tm < last)
+    def _():
+        for h in range(HALO):
+            halo_copy(h).wait_send()
+
+    for slot in range(slots):
+
+        def sent(slot=slot):
+            drain(send.at[slot, pl.ds(0, devices - 1)], send_sems.at[slot])
+
+        if slot < HALO:
+            pl.when(tm > 0)(sent)
+        elif slot < spec_dev:
+            sent()
+        else:
+            pl.when(tm == last)(sent)
+
+
+def channel_spectra(voltages, cal_gains, tm_count, chan_count):
+    inputs = voltages.shape[0]
+    spec_dev = voltages.shape[1] // NFFT
+    spectra = spec_dev * tm_count
+    devices = tm_count * chan_count
+    slots = spec_dev + HALO
+    _, chan_local, all_inputs = cal_gains.shape
+    rows = 2 * LANES // devices
     return pl.pallas_call(
-        exchange_kernel,
-        in_specs=[pl.BlockSpec(memory_space=pl.ANY)],
-        out_specs=pl.BlockSpec(memory_space=pl.ANY),
-        out_shape=jax.ShapeDtypeStruct(bins.shape, bins.dtype),
+        spectra_kernel,
+        out_shape=jax.ShapeDtypeStruct((chan_local, 2 * spectra, all_inputs), jnp.bfloat16),
         scratch_shapes=[
-            pltpu.SemaphoreType.DMA((bins.shape[0] - 1,)),
-            pltpu.SemaphoreType.DMA((bins.shape[0] - 1,)),
+            pltpu.VMEM((spec_dev + 2 * HALO, RADIX, inputs, LANES), jnp.bfloat16),
+            pltpu.VMEM((TAPS, RADIX, 8, LANES), jnp.float32),
+            pltpu.VMEM((RADIX // 2 + 1, 2, 8, LANES), jnp.float32),
+            pltpu.VMEM((RADIX, inputs, LANES), jnp.float32),
+            pltpu.VMEM((PAIRS, 2 * inputs, 2 * LANES), jnp.float32),
+            pltpu.VMEM((inputs, 2 * LANES), jnp.float32),
+            pltpu.VMEM((slots, devices, PAIRS, rows, LANES), jnp.bfloat16),
+            pltpu.VMEM((chan_count, spectra, PAIRS, rows, LANES), jnp.bfloat16),
+            pltpu.VMEM((chan_count, spectra * rows, LANES), jnp.float32),
+            pltpu.SemaphoreType.DMA((HALO,)),
+            pltpu.SemaphoreType.DMA((HALO,)),
+            pltpu.SemaphoreType.DMA((slots,)),
             pltpu.SemaphoreType.DMA,
+            pltpu.SemaphoreType.DMA((CHUNKS,)),
         ],
         compiler_params=pltpu.CompilerParams(collective_id=0, has_side_effects=True),
-        name="exchange",
-    )(bins)
-
-
-def correlate_bins_kernel(
-    bins_ref, gain_ref, delay_ref, vis_ref, power_ref,
-    cur_re, cur_im, rot_re, rot_im, far_re, far_im, w_re, w_im, rows_buf, power_buf,
-):
-    k1 = pl.program_id(0)
-    tm_count, chan_count = lax.axis_size("tm"), lax.axis_size("chan")
-    sources, _, size, lanes = bins_ref.shape
-    block = vis_ref.shape[1]
-    inputs = vis_ref.shape[4]
-    own_inputs = inputs // chan_count
-    spec_dev = lanes // own_inputs
-    spectra = spec_dev * tm_count
-
-    @pl.when(k1 == 0)
-    def _():
-        first = (lax.axis_index("tm") * chan_count + lax.axis_index("chan")) * (block * RADIX)
-        delays = delay_ref[...].T
-        norm = 1.0 / math.sqrt(inputs)
-
-        def phase(steps):
-            return (delays * steps % NFFT).astype(jnp.float32) * (2.0 * math.pi / NFFT)
-
-        cur_re[...] = jnp.cos(phase(first)) * norm
-        cur_im[...] = -jnp.sin(phase(first)) * norm
-        rot_re[...] = jnp.cos(phase(1))
-        rot_im[...] = -jnp.sin(phase(1))
-        far_re[...] = jnp.cos(phase(RADIX))
-        far_im[...] = -jnp.sin(phase(RADIX))
-
-    rows = 16
-
-    def advance(chunk, carry):
-        at = pl.ds(pl.multiple_of(chunk * rows, rows), rows)
-        c_re, c_im = cur_re[at, :], cur_im[at, :]
-        r_re, r_im = rot_re[at, :], rot_im[at, :]
-        cur_re[at, :] = c_re * r_re - c_im * r_im
-        cur_im[at, :] = c_re * r_im + c_im * r_re
-        r_re, r_im = far_re[at, :], far_im[at, :]
-        for q in range(block):
-            w_re[q, at, :] = c_re.astype(jnp.bfloat16)
-            w_im[q, at, :] = c_im.astype(jnp.bfloat16)
-            if q + 1 < block:
-                c_re, c_im = c_re * r_re - c_im * r_im, c_re * r_im + c_im * r_re
-        return carry
-
-    lax.fori_loop(0, inputs // rows, advance, 0, unroll=True)
-
-    received = bins_ref[...].astype(jnp.float32).reshape(sources * size, lanes)
-    for part in range(lanes // LANES):
-        rows_buf[part] = received[:, part * LANES : (part + 1) * LANES]
-    mirror = jnp.where(k1 >= RADIX // 2, size // 2, 0)
-
-    def gathered(row):
-        parts = []
-        for chan in range(chan_count):
-            at = pl.ds(chan * tm_count * size + mirror + row, tm_count, stride=size)
-            pieces = [rows_buf[part, at, :] for part in range(lanes // LANES)]
-            parts.append(jnp.concatenate(pieces, axis=1))
-        return jnp.concatenate(
-            [
-                jnp.concatenate([p[:, s * own_inputs : (s + 1) * own_inputs] for p in parts], axis=1)
-                for s in range(spec_dev)
-            ],
-            axis=0,
-        )
-
-    g_re_all, g_im_all = gain_ref[0, :, 0], gain_ref[1, :, 0]
-    for q in range(block):
-        a_re, a_im = gathered(q), gathered(block + q)
-        g_re, g_im = g_re_all[q], g_im_all[q]
-        cal_re = (g_re * a_re - g_im * a_im).astype(jnp.bfloat16)
-        cal_im = (g_re * a_im + g_im * a_re).astype(jnp.bfloat16)
-        stacked = jnp.concatenate([cal_re, cal_im], axis=0)
-        flipped = jnp.concatenate([cal_im, -cal_re], axis=0)
-        over_time = (((0,), (0,)), ((), ()))
-        for part, left in enumerate((stacked, flipped)):
-            vis = lax.dot_general(left, stacked, over_time, preferred_element_type=jnp.float32)
-            vis_ref[part, q, 0] = (vis * (1.0 / spectra)).astype(jnp.bfloat16)
-        by_re = jnp.dot(stacked, w_re[q], preferred_element_type=jnp.float32)
-        by_im = jnp.dot(stacked, w_im[q], preferred_element_type=jnp.float32)
-        beam_re = by_re[:spectra] - by_im[spectra:]
-        beam_im = by_re[spectra:] + by_im[:spectra]
-        power = beam_re * beam_re + beam_im * beam_im
-        for part in range(power.shape[1] // LANES):
-            cols = slice(part * LANES, (part + 1) * LANES)
-            power_buf[q, part] = power[:, cols]
-            in_order = [
-                power_buf[q, part, pl.ds(t, spec_dev, stride=tm_count), :] for t in range(tm_count)
-            ]
-            power_ref[q, 0, :, cols] = jnp.concatenate(in_order, axis=0).astype(jnp.bfloat16)
-
-
-def correlate_bins(bins, beam_delays, cal_gains):
-    sources, half, size, lanes = bins.shape
-    _, chan_local, inputs = cal_gains.shape
-    beams = beam_delays.shape[0]
-    block = chan_local // RADIX
-    spectra = sources * lanes // inputs
-    table = pltpu.VMEM((inputs, beams), jnp.float32)
-    vis, power = pl.pallas_call(
-        correlate_bins_kernel,
-        grid=(RADIX,),
-        in_specs=[
-            pl.BlockSpec(
-                (sources, 1, size, lanes),
-                lambda k: (0, jnp.where(k > half, RADIX - k, lax.rem(k, half)), 0, 0),
-            ),
-            pl.BlockSpec((2, block, 1, 1, inputs), lambda k: (0, 0, k, 0, 0)),
-            pl.BlockSpec((beams, inputs), lambda k: (0, 0)),
-        ],
-        out_specs=[
-            pl.BlockSpec((2, block, 1, inputs, inputs), lambda k: (0, 0, k, 0, 0)),
-            pl.BlockSpec((block, 1, spectra, beams), lambda k: (0, k, 0, 0)),
-        ],
-        out_shape=[
-            jax.ShapeDtypeStruct((2, block, RADIX, inputs, inputs), jnp.bfloat16),
-            jax.ShapeDtypeStruct((block, RADIX, spectra, beams), jnp.bfloat16),
-        ],
-        scratch_shapes=[table] * 6
-        + [pltpu.VMEM((block, inputs, beams), jnp.bfloat16)] * 2
-        + [
-            pltpu.VMEM((lanes // LANES, sources * size, LANES), jnp.float32),
-            pltpu.VMEM((block, beams // LANES, spectra, LANES), jnp.float32),
-        ],
-        compiler_params=pltpu.CompilerParams(dimension_semantics=("arbitrary",)),
-        name="correlate",
-    )(bins, cal_gains.reshape(2, block, RADIX, 1, inputs), beam_delays)
-    return (
-        vis.reshape(2, chan_local, inputs, inputs),
-        power.reshape(chan_local, spectra, beams),
-    )
+        name="spectra",
+    )(voltages, window_table(), twiddle_table(), second_stage(devices), cal_gains)
 
 
 def correlate_kernel(
@@ -434,17 +562,99 @@
     )(spectra, cal_gains, beam_delays)
 
 
+def beams_kernel(
+    cal_ref, delay_ref, vis_ref, power_ref, cur_re, cur_im, rot_re, rot_im, w_re, w_im
+):
+    step = pl.program_id(0)
+    block = cal_ref.shape[0]
+    spectra = cal_ref.shape[1] // 2
+    inputs = cal_ref.shape[2]
+    beams = delay_ref.shape[0]
+
+    @pl.when(step == 0)
+    def _():
+        chan_count = lax.axis_size("chan")
+        first = (lax.axis_index("tm") * chan_count + lax.axis_index("chan")) * (
+            block * pl.num_programs(0)
+        )
+        delays = delay_ref[...].T
+        start = (delays * first % NFFT).astype(jnp.float32) * (2.0 * math.pi / NFFT)
+        turn = delays.astype(jnp.float32) * (2.0 * math.pi / NFFT)
+        norm = 1.0 / math.sqrt(inputs)
+        cur_re[...] = jnp.cos(start) * norm
+        cur_im[...] = -jnp.sin(start) * norm
+        rot_re[...] = jnp.cos(turn)
+        rot_im[...] = -jnp.sin(turn)
+
+    rows = 16
+
+    def advance(chunk, carry):
+        at = pl.ds(pl.multiple_of(chunk * rows, rows), rows)
+        c_re, c_im = cur_re[at, :], cur_im[at, :]
+        r_re, r_im = rot_re[at, :], rot_im[at, :]
+        for c in range(block):
+            w_re[c, at, :] = c_re.astype(jnp.bfloat16)
+            w_im[c, at, :] = c_im.astype(jnp.bfloat16)
+            c_re, c_im = c_re * r_re - c_im * r_im, c_re * r_im + c_im * r_re
+        cur_re[at, :] = c_re
+        cur_im[at, :] = c_im
+        return carry
+
+    lax.fori_loop(0, inputs // rows, advance, 0, unroll=True)
+
+    for c in range(block):
+        cal_re, cal_im = cal_ref[c, :spectra], cal_ref[c, spectra:]
+        stacked = jnp.concatenate([cal_re, cal_im], axis=0)
+        flipped = jnp.concatenate([cal_im, -cal_re], axis=0)
+        over_time = (((0,), (0,)), ((), ()))
+        for part, left in enumerate((stacked, flipped)):
+            vis = lax.dot_general(left, stacked, over_time, preferred_element_type=jnp.float32)
+            vis_ref[part, c] = (vis * (1.0 / spectra)).astype(jnp.bfloat16)
+        by_re = jnp.dot(stacked, w_re[c], preferred_element_type=jnp.float32)
+        by_im = jnp.dot(stacked, w_im[c], preferred_element_type=jnp.float32)
+        beam_re = by_re[:spectra] - by_im[spectra:]
+        beam_im = by_re[spectra:] + by_im[:spectra]
+        power_ref[c] = (beam_re * beam_re + beam_im * beam_im).astype(jnp.bfloat16)
+
+
+def beams_and_visibilities(calibrated, beam_delays):
+    chan_local, rows, inputs = calibrated.shape
+    spectra_total = rows // 2
+    beams = beam_delays.shape[0]
+    block = math.gcd(chan_local, 8)
+    table = pltpu.VMEM((inputs, beams), jnp.float32)
+    return pl.pallas_call(
+        beams_kernel,
+        grid=(chan_local // block,),
+        in_specs=[
+            pl.BlockSpec((block, rows, inputs), lambda g: (g, 0, 0)),
+            pl.BlockSpec((beams, inputs), lambda g: (0, 0)),
+        ],
+        out_specs=[
+            pl.BlockSpec((2, block, inputs, inputs), lambda g: (0, g, 0, 0)),
+            pl.BlockSpec((block, spectra_total, beams), lambda g: (g, 0, 0)),
+        ],
+        out_shape=[
+            jax.ShapeDtypeStruct((2, chan_local, inputs, inputs), jnp.bfloat16),
+            jax.ShapeDtypeStruct((chan_local, spectra_total, beams), jnp.bfloat16),
+        ],
+        scratch_shapes=[table] * 4 + [pltpu.VMEM((block, inputs, beams), jnp.bfloat16)] * 2,
+        compiler_params=pltpu.CompilerParams(dimension_semantics=("arbitrary",)),
+        name="beams",
+    )(calibrated, beam_delays)
+
+
 def shards(voltages, beam_delays, cal_gains):
     inp_dev = voltages.shape[0]
     spec_dev = voltages.shape[1] // NFFT
     tm_count = lax.axis_size("tm")
     chan_count = lax.axis_size("chan")
     spectra_total = spec_dev * tm_count
+    devices = tm_count * chan_count
+    if 2 * inp_dev == LANES and spec_dev >= HALO and tm_count > 1 and 2 * LANES == 16 * devices:
+        calibrated = channel_spectra(voltages, cal_gains, tm_count, chan_count)
+        return beams_and_visibilities(calibrated, beam_delays)
     halo = shifted(voltages[:, : (TAPS - 1) * NFFT].astype(jnp.bfloat16), "tm", -1)
-    devices = tm_count * chan_count
-    if CH % (4 * RADIX * devices) == 0:
-        bins = exchange(channelize(voltages, halo, devices))
-        return correlate_bins(bins, beam_delays, cal_gains)
     half = LANES // 2
     bins = channelize(voltages, halo, half).reshape(RADIX // 2, half, 2, 2, spec_dev, inp_dev)
     plain, mirror = bins[:, :, 0], bins[:, :, 1]

time: 142 us -> 102 us (0.72)
  the two profiles are of different devices: /device:TPU:9 before, /device:TPU:0 now
where the time goes in v1:
time: 102 us
  Pallas kernels  102 us (100%)
    pallas_call x1, Pallas kernels, channel_spectra(): pl.pallas_call(spectra_kernel, out_shape=jax.ShapeDtypeStruct((chan_local...  77.7 us
    pallas_call x1, Pallas kernels, beams_and_visibilities(): pl.pallas_call(beams_kernel, grid=(chan_local // block,), in_specs=[pl.Bl...  23.9 us

profile of v1, /device:TPU:0, one launch (start us, length us, event | category | flops | bytes accessed | tf_op | source)
XLA Modules:
  0.0 102.3 jit_solution(11126807079282663264)
XLA Ops:
  0.6 77.7 %spectra.1.cal_ref = bf16[128,32,256]{2,1,0:T(8,128)(2,1)} custom-call(s32[64,16384]{1,0:T(8,128)} %volt_ref.1, f32[4,32,128]{2,1,0:T(8,128)} %constant.6.clone.window_ref, f32[17,2,128]{2,1,0:T(2,128)} %constant.7.clone.twiddle_ref, bf16[3,2,256,256]{3,2,1,0:T(8,128)(2,1)} %constant.8.clone.dft_ref, f32[2,128,256]{2,1,0:T(8,128)} %gain_ref.1), custom_call_target="tpu_custom_call" | custom-call | tf_op jit(solution)/shard_map/spectra/pallas_call | solution.py:454
  78.4 23.9 %beams.1 = (bf16[2,128,256,256]{3,2,1,0:T(8,128)(2,1)}, bf16[128,16,256]{2,1,0:T(8,128)(2,1)}) custom-call(bf16[128,32,256]{2,1,0:T(8,128)(2,1)} %spectra.1.cal_ref, s32[256,256]{1,0:T(8,128)} %delay_ref.1), custom_call_target="tpu_custom_call" | custom-call | tf_op jit(solution)/shard_map/beams/pallas_call | solution.py:626
